TPU v7x, 32 devices: a whole 2x2x4 slice. The times are simulated.
32 devices in a mesh: rows: 8 (over y, x, core), tp: 4 (over z).
Axes of the slice: x: 2, y: 2, z: 4, core: 2. Of those that a mesh axis runs over, the one named last changes fastest.
Arguments:
- hidden: bfloat16 [2048, 8, 1024], P('tp', 'rows'), may hold values from -6 to 6
- cotangent: bfloat16 [2048, 8, 1024], P('tp', 'rows'), may hold values from -6 to 6
- pair_lengths: int32 [8, 12], P('rows'), may hold values from 1 to 512, 2048 in all within a row
- w_qkv: bfloat16 [3, 1024, 1024], P(None, 'rows', 'tp'), may hold values from -0.1875 to 0.1875
- qkv_bias: bfloat16 [3, 1024], P(None, 'tp'), may hold values from -3 to 3
- w_out: bfloat16 [1024, 1024], P('tp', 'rows'), may hold values from -1.5 to 1.5
- w_up: bfloat16 [1024, 4096], P('rows', 'tp'), may hold values from -0.1875 to 0.1875
- up_bias: bfloat16 [4096], P('tp'), may hold values from -3 to 3
- w_down: bfloat16 [4096, 1024], P('tp', 'rows'), may hold values from -0.09375 to 0.09375
- resid_bias: bfloat16 [2, 1024], replicated, may hold values from -3 to 3
- norm_gain: bfloat16 [2, 1024], replicated, may hold values from 0.5 to 1.5
- norm_bias: bfloat16 [2, 1024], replicated, may hold values from -2 to 2
- prefix_keys: bfloat16 [64, 1024], P(None, 'tp'), may hold values from -6 to 6
- prefix_values: bfloat16 [64, 1024], P(None, 'tp'), may hold values from -6 to 6
Outputs:
- result: bfloat16 [2048, 8, 1024], P('tp', 'rows')
- grad_input: float32 [2048, 8, 1024], P('tp', 'rows')
- key_total: float32 [64, 1024], P(None, 'tp')
- value_total: float32 [64, 1024], P(None, 'tp')
Inputs may be any that keep to these rules, and one draw needn't show every extreme that they name: Each row of pair_lengths holds 11 pair lengths followed by the length of the trailing pad; a row's entries sum to 2048 and its largest is exactly 512.
All inputs are finite; a program needn't handle non-finite values.
Results may differ from a plain program's by a relative error of at most 0.015.
Values may be sent and summed in bfloat16 or wider, within the bound.
No kernel may reach another device: no remote copies, remote signals or barrier semaphores. Data moves between devices by JAX's collectives and lax.ppermute only.
A program may use at most 128 MiB of HBM per device.

v0:
```python
from functools import partial
import jax
import jax.numpy as jnp
from jax import lax
from jax.sharding import PartitionSpec as P

HEAD_DIM = 64
PREFIX = 64
SEQ = 2048
QBLOCK = 512
EPS = 1e-05
NEG = -1e30


def layer_norm(values, gain, shift):
    mean = jnp.mean(values, axis=-1, keepdims=True)
    centred = values - mean
    variance = jnp.mean(centred * centred, axis=-1, keepdims=True)
    return centred * lax.rsqrt(variance + EPS) * gain + shift


def norm_back(values, gain, shift, grad):
    unused, pull = jax.vjp(lambda inner: layer_norm(inner, gain, shift), values)
    return pull(grad)[0]


def segment_ids(pair_lengths):
    ends = jnp.cumsum(pair_lengths, axis=-1)
    place = jnp.arange(SEQ, dtype=jnp.int32)
    return jnp.sum((place[None, :, None] >= ends[:, None, :]).astype(jnp.int32), axis=-1)


def block_scores(query_block, keys_all, seg_block, key_seg, pad_id):
    scale = HEAD_DIM ** (-0.5)
    scores = (
        jnp.einsum("qhd,khd->hqk", query_block, keys_all, preferred_element_type=jnp.float32)
        * scale
    )
    is_prefix = jnp.arange(key_seg.shape[0], dtype=jnp.int32) < PREFIX
    allowed = is_prefix[None, :] | (key_seg[None, :] == seg_block[:, None]) & (
        seg_block[:, None] != pad_id
    )
    return jnp.where(allowed[None], scores, NEG)


def row_parts(packed_row, seg_row, key_prefix, value_prefix):
    keys_all = jnp.concatenate([key_prefix, packed_row[:, 1]], axis=0)
    values_all = jnp.concatenate([value_prefix, packed_row[:, 2]], axis=0)
    key_seg = jnp.concatenate([jnp.full((PREFIX,), -1, jnp.int32), seg_row])
    return (packed_row[:, 0], keys_all, values_all, key_seg)


def attend_row(packed_row, seg_row, key_prefix, value_prefix, pad_id):
    queries, keys_all, values_all, key_seg = row_parts(
        packed_row, seg_row, key_prefix, value_prefix
    )
    blocks = SEQ // QBLOCK
    heads_here = queries.shape[1]

    def one(args):
        query_block, seg_block = args
        scores = block_scores(query_block, keys_all, seg_block, key_seg, pad_id)
        peak = jnp.max(scores, axis=-1, keepdims=True)
        expo = jnp.exp(scores - peak)
        total = jnp.sum(expo, axis=-1, keepdims=True)
        probs = (expo / total).astype(jnp.bfloat16)
        mixed = jnp.einsum("hqk,khd->qhd", probs, values_all, preferred_element_type=jnp.float32)
        return (mixed.astype(jnp.bfloat16), (peak + jnp.log(total))[..., 0])

    mixed, logsum = lax.map(
        one,
        (queries.reshape(blocks, QBLOCK, heads_here, HEAD_DIM), seg_row.reshape(blocks, QBLOCK)),
    )
    return (mixed.reshape(SEQ, heads_here * HEAD_DIM), logsum)


def attend_back(packed_row, seg_row, grad_row, logsum, key_prefix, value_prefix, pad_id):
    queries, keys_all, values_all, key_seg = row_parts(
        packed_row, seg_row, key_prefix, value_prefix
    )
    blocks = SEQ // QBLOCK
    heads_here = queries.shape[1]
    scale = HEAD_DIM ** (-0.5)

    def one(carry, args):
        key_acc, value_acc = carry
        query_block, seg_block, grad_block, sums = args
        scores = block_scores(query_block, keys_all, seg_block, key_seg, pad_id)
        probs = jnp.exp(scores - sums[:, :, None])
        dprobs = jnp.einsum(
            "qhd,khd->hqk", grad_block, values_all, preferred_element_type=jnp.float32
        )
        inner = jnp.sum(probs * dprobs, axis=-1, keepdims=True)
        dscores = (probs * (dprobs - inner)).astype(jnp.bfloat16)
        query_grad = (
            jnp.einsum("hqk,khd->qhd", dscores, keys_all, preferred_element_type=jnp.float32)
            * scale
        )
        key_acc = (
            key_acc
            + jnp.einsum("hqk,qhd->khd", dscores, query_block, preferred_element_type=jnp.float32)
            * scale
        )
        value_acc = value_acc + jnp.einsum(
            "hqk,qhd->khd",
            probs.astype(jnp.bfloat16),
            grad_block,
            preferred_element_type=jnp.float32,
        )
        return ((key_acc, value_acc), query_grad.astype(jnp.bfloat16))

    start_acc = (jnp.zeros(keys_all.shape, jnp.float32), jnp.zeros(values_all.shape, jnp.float32))
    inputs = (
        queries.reshape(blocks, QBLOCK, heads_here, HEAD_DIM),
        seg_row.reshape(blocks, QBLOCK),
        grad_row.reshape(blocks, QBLOCK, heads_here, HEAD_DIM),
        logsum,
    )
    (key_acc, value_acc), query_grads = lax.scan(one, start_acc, inputs)
    grad_packed = jnp.stack(
        [
            query_grads.reshape(SEQ, heads_here, HEAD_DIM),
            key_acc[PREFIX:].astype(jnp.bfloat16),
            value_acc[PREFIX:].astype(jnp.bfloat16),
        ],
        axis=1,
    )
    return (grad_packed, key_acc[:PREFIX], value_acc[:PREFIX])


def collect(w_qkv, w_out, w_up, w_down):
    return (
        lax.all_gather(w_qkv, "rows", axis=1, tiled=True),
        lax.all_gather(w_out, "rows", axis=1, tiled=True),
        lax.all_gather(w_up, "rows", axis=0, tiled=True),
        lax.all_gather(w_down, "rows", axis=1, tiled=True),
    )


def project_inputs(hidden, qkv_full, qkv_shift):
    piece = lax.all_gather(hidden, "tp", axis=0, tiled=True)
    mixed = (
        jnp.einsum("nrd,jde->nrje", piece, qkv_full, preferred_element_type=jnp.float32) + qkv_shift
    )
    return mixed.astype(jnp.bfloat16).reshape(piece.shape[0], piece.shape[1], -1)


def expand(normed_low, up_full, up_shift):
    return (
        jnp.einsum(
            "nrd,df->nrf",
            lax.all_gather(normed_low, "tp", axis=0, tiled=True),
            up_full,
            preferred_element_type=jnp.float32,
        )
        + up_shift
    )


def mix_heads(mixed, out_full):
    return lax.psum_scatter(
        jnp.einsum("nrk,kd->nrd", mixed, out_full, preferred_element_type=jnp.float32),
        "tp",
        scatter_dimension=0,
        tiled=True,
    )


def reduce_down(active, down_full):
    return lax.psum_scatter(
        jnp.einsum("nrf,fd->nrd", active, down_full, preferred_element_type=jnp.float32),
        "tp",
        scatter_dimension=0,
        tiled=True,
    )


def output_back(grad_low, down_full, expanded):
    grad_active = jnp.einsum(
        "nrd,fd->nrf",
        lax.all_gather(grad_low, "tp", axis=0, tiled=True),
        down_full,
        preferred_element_type=jnp.float32,
    )
    unused, pull = jax.vjp(partial(jax.nn.gelu, approximate=False), expanded)
    return pull(grad_active)[0].astype(jnp.bfloat16)


def up_back(grad_hidden, up_full):
    return lax.psum_scatter(
        jnp.einsum("nrf,df->nrd", grad_hidden, up_full, preferred_element_type=jnp.float32),
        "tp",
        scatter_dimension=0,
        tiled=True,
    )


def mixing_back(grad_low, out_full):
    return jnp.einsum(
        "nrd,kd->nrk",
        lax.all_gather(grad_low, "tp", axis=0, tiled=True),
        out_full,
        preferred_element_type=jnp.float32,
    ).astype(jnp.bfloat16)


def input_back(grad_packed, qkv_full, local_rows):
    piece = grad_packed
    piece = piece.reshape(lax.axis_size("tp") * local_rows, piece.shape[1], 3, -1)
    return lax.psum_scatter(
        jnp.einsum("nrje,jde->nrd", piece, qkv_full, preferred_element_type=jnp.float32).astype(
            jnp.bfloat16
        ),
        "tp",
        scatter_dimension=0,
        tiled=True,
    ).astype(jnp.float32)


def body(
    hidden,
    cotangent,
    pair_lengths,
    w_qkv,
    qkv_bias,
    w_out,
    w_up,
    up_bias,
    w_down,
    resid_bias,
    norm_gain,
    norm_bias,
    prefix_keys,
    prefix_values,
):
    local_rows = hidden.shape[0]
    row_count = hidden.shape[1]
    width = w_qkv.shape[2]
    heads_here = width // HEAD_DIM
    pad_id = pair_lengths.shape[1] - 1
    seg = segment_ids(pair_lengths)
    shifts = resid_bias.astype(jnp.float32)
    gains = norm_gain.astype(jnp.float32)
    offsets = norm_bias.astype(jnp.float32)
    qkv_shift = qkv_bias.astype(jnp.float32)
    up_shift = up_bias.astype(jnp.float32)
    key_prefix = prefix_keys.reshape(PREFIX, heads_here, HEAD_DIM)
    value_prefix = prefix_values.reshape(PREFIX, heads_here, HEAD_DIM)

    def heads_of(packed):
        return jnp.moveaxis(packed.reshape(SEQ, row_count, 3, heads_here, HEAD_DIM), 1, 0)

    qkv_full, out_full, up_full, down_full = collect(w_qkv, w_out, w_up, w_down)
    packed = project_inputs(hidden, qkv_full, qkv_shift)
    mixed, logsum = lax.map(
        lambda args: attend_row(args[0], args[1], key_prefix, value_prefix, pad_id),
        (heads_of(packed), seg),
    )
    attended = mix_heads(jnp.moveaxis(mixed, 0, 1), out_full)
    first = hidden.astype(jnp.float32) + attended + shifts[0]
    normed = layer_norm(first, gains[0], offsets[0])
    normed_low = normed.astype(jnp.bfloat16)
    expanded = expand(normed_low, up_full, up_shift)
    active = jax.nn.gelu(expanded, approximate=False).astype(jnp.bfloat16)
    second = normed + reduce_down(active, down_full) + shifts[1]
    result = layer_norm(second, gains[1], offsets[1])
    qkv_full, out_full, up_full, down_full = collect(w_qkv, w_out, w_up, w_down)
    packed = project_inputs(hidden, qkv_full, qkv_shift)
    expanded = expand(normed_low, up_full, up_shift)
    grad_second = norm_back(second, gains[1], offsets[1], cotangent.astype(jnp.float32))
    grad_hidden = output_back(grad_second.astype(jnp.bfloat16), down_full, expanded)
    grad_normed = up_back(grad_hidden, up_full) + grad_second
    grad_first = norm_back(first, gains[0], offsets[0], grad_normed)
    grad_mixed = mixing_back(grad_first.astype(jnp.bfloat16), out_full)
    grad_rows = jnp.moveaxis(grad_mixed, 1, 0).reshape(row_count, SEQ, heads_here, HEAD_DIM)
    grad_packed, key_grads, value_grads = lax.map(
        lambda args: attend_back(
            args[0], args[1], args[2], args[3], key_prefix, value_prefix, pad_id
        ),
        (heads_of(packed), seg, grad_rows, logsum),
    )
    grad_packed = jnp.moveaxis(grad_packed, 0, 1).reshape(SEQ, row_count, 3 * width)
    grad_input = input_back(grad_packed, qkv_full, local_rows) + grad_first
    key_local = jnp.sum(key_grads, axis=0).reshape(PREFIX, width)
    value_local = jnp.sum(value_grads, axis=0).reshape(PREFIX, width)
    key_total, value_total = (
        lax.psum(key_local.astype(jnp.bfloat16), "rows").astype(jnp.float32),
        lax.psum(value_local.astype(jnp.bfloat16), "rows").astype(jnp.float32),
    )
    return (result.astype(jnp.bfloat16), grad_input, key_total, value_total)


def solution(mesh):
    placed = (
        P("tp", "rows", None),
        P("tp", "rows", None),
        P("rows", None),
        P(None, "rows", "tp"),
        P(None, "tp"),
        P("tp", "rows"),
        P("rows", "tp"),
        P("tp"),
        P("tp", "rows"),
        P(),
        P(),
        P(),
        P(None, "tp"),
        P(None, "tp"),
    )
    return jax.shard_map(
        body,
        mesh=mesh,
        in_specs=placed,
        out_specs=(P("tp", "rows", None), P("tp", "rows", None), P(None, "tp"), P(None, "tp")),
        check_vma=False,
    )
```

profile of v0, /device:TPU:0, one launch (start us, length us, event | category | flops | bytes accessed | tf_op | source)
XLA Modules:
  0.0 1455.1 jit_solution(514246632856984945)
XLA Ops:
  13.4 14.6 %all_gather.32 = bf16[256,1024]{1,0:T(8,128)(2,1)} all-gather(bf16[256,128]{1,0:T(8,128)(2,1)} %param.23), channel_id=1, replica_groups=mesh['rows'=8,'tp'=4] {'rows'}, dimensions={1}, use_global_device_ids=true | all-gather | bytes 589824 | tf_op jit(solution)/shard_map/all_gather | solution.py:134
  28.0 12.3 all-gather.10.cloned.1.call-done
  40.3 82.3 %all-gather.8.cloned.1.call-done = bf16[2048,1,1024]{2,0,1:T(8,128)(2,1)} async-done(((bf16[512,1,1024]{2,0,1:T(8,128)(2,1)}), bf16[2048,1,1024]{2,0,1:T(8,128)(2,1)}) %all-gather.8.cloned.1.call-update) | async-done | bytes 4194320 | tf_op jit(solution)/shard_map/all_gather | solution.py:141
  135.6 120.9 %while.47 = (s32[]{:T(128)}, bf16[4,512,4,64]{1,3,2,0:T(8,128)(2,1)}, f32[4,4,512]{2,1,0:T(4,128)S(1)}, s32[2112]{0:T(1024)S(1)}, s32[4,512]{1,0:T(4,128)S(1)}, ...) while((s32[]{:T(128)}, ...), condition=%wide.region_5.6_spmd, body=%wide.region_2.5_spmd.sunk | while | flops 1162576384 | bytes 59005412 | solution.py:70
  137.2 8.8 fusion.120
  146.0 9.6 fusion.121
  155.6 10.2 fusion.122
  167.4 8.8 fusion.120
  176.2 9.6 fusion.121
  185.8 10.2 fusion.122
  197.6 8.8 fusion.120
  206.4 9.6 fusion.121
  215.9 10.2 fusion.122
  227.7 8.8 fusion.120
  236.5 9.6 fusion.121
  246.1 10.2 fusion.122
  264.2 142.6 %reduce-scatter.5.cloned.1.call-done = f32[512,1,1024]{2,0,1:T(8,128)} async-done(((f32[2048,1,1024]{2,0,1:T(8,128)}), f32[512,1,1024]{2,0,1:T(8,128)}) %reduce-scatter.5.cloned.1.call-update) | async-done | bytes 2097168 | tf_op jit(solution)/shard_map/reduce_scatter | solution.py:161
  412.0 24.8 %all-gather.14.cloned.1.call-done = bf16[1024,1024]{1,0:T(8,128)(2,1)} async-done(((bf16[128,1024]{1,0:T(8,128)(2,1)}), bf16[1024,1024]{1,0:T(8,128)(2,1)}) %all-gather.14.cloned.1.call-update) | async-done | bytes 2097168 | tf_op jit(solution)/shard_map/all_gather | solution.py:135
  436.9 82.8 %all-gather.12.cloned.1.call-done = bf16[2048,1,1024]{2,0,1:T(8,128)(2,1)} async-done(((bf16[512,1,1024]{2,0,1:T(8,128)(2,1)}), bf16[2048,1,1024]{2,0,1:T(8,128)(2,1)}) %all-gather.12.cloned.1.call-update) | async-done | bytes 4194320 | tf_op jit(solution)/shard_map/all_gather | solution.py:152
  519.6 25.3 %fusion.38 = (f32[2048,1024]{1,0:T(8,128)}, f32[2048,1024]{1,0:T(8,128)}) fusion(f32[1024]{0:T(1024)S(1)} %convert_element_type.117, bf16[1024,1024]{1,0:T(8,128)(2,1)} %all-gather.14.cloned.1.call-done, bf16[2048,1,1024]{2,0,1:T(8,128)(2,1)} %all-gather.12.cloned.1.call-done), kind=kOutput, calls=%fused_computation.53 | convolution fusion | flops 4427087872 | bytes 23072768 | tf_op jit(solution)/shard_map/nrd,df->nrf/dot_general | solution.py:150
  548.0 14.1 convolution_bitcast_fusion.1
  562.6 144.3 %reduce-scatter.7.cloned.1.call-done = f32[512,1,1024]{2,0,1:T(8,128)} async-done(((f32[2048,1,1024]{2,0,1:T(8,128)}), f32[512,1,1024]{2,0,1:T(8,128)}) %reduce-scatter.7.cloned.1.call-update) | async-done | bytes 2097168 | tf_op jit(solution)/shard_map/reduce_scatter | solution.py:170
  715.0 81.4 %all-gather.18.cloned.1.call-done = bf16[2048,1,1024]{2,0,1:T(8,128)(2,1)} async-done(((bf16[512,1,1024]{2,0,1:T(8,128)(2,1)}), bf16[2048,1,1024]{2,0,1:T(8,128)(2,1)}) %all-gather.18.cloned.1.call-update) | async-done | bytes 4194320 | tf_op jit(solution)/shard_map/all_gather | solution.py:181
  796.4 18.0 %convolution_bitcast_fusion = f32[2048,1,1024]{2,0,1:T(8,128)} fusion(bf16[1024,1024]{1,0:T(8,128)(2,1)} %all-gather.14.cloned.1.call-done, f32[2048,1024]{1,0:T(8,128)} %get-tuple-element.325, f32[2048,1024]{1,0:T(8,128)} %get-tuple-element.326, f32[1024]{0:T(1024)S(1)} %convert_element_type.117, bf16[1024,1024]{1,0:T(8,128)(2,1)} %all-gather.16.cloned.1.call-done, ...), kind=kOutput, calls=%fused_computation.71 | convolution fusion | flops 8621391872 | bytes 33558528 | tf_op jit(solution)/shard_map/nrf,df->nrd/dot_general | solution.py:191
  814.5 143.2 %reduce-scatter.9.cloned.1.call-done = f32[512,1,1024]{2,0,1:T(8,128)} async-done(((f32[2048,1,1024]{2,0,1:T(8,128)}), f32[512,1,1024]{2,0,1:T(8,128)}) %reduce-scatter.9.cloned.1.call-update) | async-done | bytes 2097168 | tf_op jit(solution)/shard_map/reduce_scatter | solution.py:190
  965.8 81.4 %all-gather.20.cloned.1.call-done = bf16[2048,1,1024]{2,0,1:T(8,128)(2,1)} async-done(((bf16[512,1,1024]{2,0,1:T(8,128)(2,1)}), bf16[2048,1,1024]{2,0,1:T(8,128)(2,1)}) %all-gather.20.cloned.1.call-update) | async-done | bytes 4194320 | tf_op jit(solution)/shard_map/all_gather | solution.py:201
  1061.5 239.9 %while.48 = (s32[]{:T(128)}, f32[2112,4,64]{0,2,1:T(8,128)}, f32[2112,4,64]{0,2,1:T(8,128)}, bf16[4,512,4,64]{1,3,2,0:T(8,128)(2,1)}, bf16[4,512,4,64]{1,3,2,0:T...) while((s32[]{:T(128)}, f32[2112,4,64]{0,2,1:T(8,128)}, ...), condition=%wide.region_19.20_spmd.clone, body=%wide.region_17.19_spmd.clone.sunk | while | flops 2813379072 | bytes 179895344 | solution.py:119
  1063.1 9.3 fusion.132
  1072.5 12.5 multiply_reduce_fusion.6
  1084.9 15.5 %multiply_convert_fusion.4 = bf16[4,512,2112]{1,2,0:T(8,128)(2,1)} fusion(f32[4,512,2112]{1,2,0:T(8,128)} %get-tuple-element.451, f32[4,512,2112]{1,2,0:T(8,128)} %fusion.132, f32[4,512]{1,0:T(4,128)S(1)} %get-tuple-element.452), kind=kLoop, calls=%fused_computation.20.clone.1 | loop fusion | flops 12976128 | bytes 43261952 | tf_op jit(solution)/shard_map/while/body/eval_jaxpr/while/body/eval_jaxpr/convert_element_type | solution.py:94
  1110.3 10.2 fusion.134
  1122.1 9.3 fusion.132
  1131.5 12.5 multiply_reduce_fusion.6
  1143.9 15.5 %multiply_convert_fusion.4 = bf16[4,512,2112]{1,2,0:T(8,128)(2,1)} fusion(f32[4,512,2112]{1,2,0:T(8,128)} %get-tuple-element.451, f32[4,512,2112]{1,2,0:T(8,128)} %fusion.132, f32[4,512]{1,0:T(4,128)S(1)} %get-tuple-element.452), kind=kLoop, calls=%fused_computation.20.clone.1 | loop fusion | flops 12976128 | bytes 43261952 | tf_op jit(solution)/shard_map/while/body/eval_jaxpr/while/body/eval_jaxpr/convert_element_type | solution.py:94
  1159.4 8.2 fusion.133
  1169.9 10.8 fusion.134
  1182.4 9.3 fusion.132
  1191.7 12.5 multiply_reduce_fusion.6
  1204.1 15.5 %multiply_convert_fusion.4 = bf16[4,512,2112]{1,2,0:T(8,128)(2,1)} fusion(f32[4,512,2112]{1,2,0:T(8,128)} %get-tuple-element.451, f32[4,512,2112]{1,2,0:T(8,128)} %fusion.132, f32[4,512]{1,0:T(4,128)S(1)} %get-tuple-element.452), kind=kLoop, calls=%fused_computation.20.clone.1 | loop fusion | flops 12976128 | bytes 43261952 | tf_op jit(solution)/shard_map/while/body/eval_jaxpr/while/body/eval_jaxpr/convert_element_type | solution.py:94
  1219.7 8.2 fusion.133
  1230.2 10.8 fusion.134
  1242.6 9.3 fusion.132
  1251.9 12.5 multiply_reduce_fusion.6
  1264.4 15.5 %multiply_convert_fusion.4 = bf16[4,512,2112]{1,2,0:T(8,128)(2,1)} fusion(f32[4,512,2112]{1,2,0:T(8,128)} %get-tuple-element.451, f32[4,512,2112]{1,2,0:T(8,128)} %fusion.132, f32[4,512]{1,0:T(4,128)S(1)} %get-tuple-element.452), kind=kLoop, calls=%fused_computation.20.clone.1 | loop fusion | flops 12976128 | bytes 43261952 | tf_op jit(solution)/shard_map/while/body/eval_jaxpr/while/body/eval_jaxpr/convert_element_type | solution.py:94
  1279.9 8.2 fusion.133
  1290.4 10.8 fusion.134
  1320.3 44.5 %all-reduce.4.cloned.1.call-done = (bf16[64,256]{1,0:T(8,128)(2,1)}, bf16[64,256]{1,0:T(8,128)(2,1)}) async-done(((bf16[64,256]{1,0:T(8,128)(2,1)}, bf16[64,256]{1,0:T(8,128)(2,1)}), (bf16[64,256]{1,0:T(8,128)(2,1)}, bf16[64,256]{1,0:T(8,128)(2,1)})) %all-reduce.4.cloned.1.call-update) | async-done | bytes 65552 | tf_op jit(solution)/shard_map/psum | solution.py:287
  1367.5 75.6 %reduce-scatter.11.cloned.1.call-done = bf16[512,1,1024]{2,0,1:T(8,128)(2,1)} async-done(((bf16[2048,1,1024]{2,0,1:T(8,128)(2,1)}), bf16[512,1,1024]{2,0,1:T(8,128)(2,1)}) %reduce-scatter.11.cloned.1.call-update) | async-done | bytes 1048592 | tf_op jit(solution)/shard_map/reduce_scatter | solution.py:210
  (178 shorter events, 121.9 us)
Async XLA Ops:
  7.2 33.1 %all-gather.10.cloned.1.call-start = ((), (), s32[]{:S(2)}) async-start(), calls=%async_computation.5 | async-start | bytes 1769472 | tf_op jit(solution)/shard_map/all_gather | solution.py:133
  9.0 113.6 %all-gather.8.cloned.1.call-start = ((), (), s32[]{:S(2)}) async-start(), calls=%async_computation.4 | async-start | bytes 5242880 | tf_op jit(solution)/shard_map/all_gather | solution.py:141
  9.7 397.0 %reduce-scatter.5.cloned.1.call-start = ((), (), s32[]{:S(2)}) async-start(), calls=%async_computation.6 | async-start | bytes 10485760 | tf_op jit(solution)/shard_map/reduce_scatter | solution.py:161
  256.5 2.4 copy-start.12
  263.4 0.7 copy-start.16
  263.4 0.7 copy-start.17
  263.4 0.7 copy-start.18
  263.4 143.3 %copy-start.10 = (bf16[512,1,1024]{2,0,1:T(8,128)(2,1)S(1)}, bf16[512,1,1024]{2,0,1:T(8,128)(2,1)}, u32[]{:S(2)}) copy-start(bf16[512,1,1024]{2,0,1:T(8,128)(2,1)} %param.18) | copy-start | bytes 3145732
  263.4 173.4 %all-gather.14.cloned.1.call-start = ((), (), s32[]{:S(2)}) async-start(), calls=%async_computation.8 | async-start | bytes 2359296 | tf_op jit(solution)/shard_map/all_gather | solution.py:135
  264.0 255.6 %all-gather.12.cloned.1.call-start = ((), (), s32[]{:S(2)}) async-start(), calls=%async_computation.7 | async-start | bytes 5242880 | tf_op jit(solution)/shard_map/all_gather | solution.py:152
  408.7 1.3 copy-start.1
  408.7 3.3 copy-start.19
  411.4 136.6 %all-gather.16.cloned.1.call-start = ((), (), s32[]{:S(2)}) async-start(), calls=%async_computation.9 | async-start | bytes 2359296 | tf_op jit(solution)/shard_map/all_gather | solution.py:136
  412.0 295.0 %reduce-scatter.7.cloned.1.call-start = ((), (), s32[]{:S(2)}) async-start(), calls=%async_computation.10 | async-start | bytes 10485760 | tf_op jit(solution)/shard_map/reduce_scatter | solution.py:170
  562.2 147.7 %copy-start.11 = (bf16[512,1,1024]{2,0,1:T(8,128)(2,1)S(1)}, bf16[512,1,1024]{2,0,1:T(8,128)(2,1)}, u32[]{:S(2)}) copy-start(bf16[512,1,1024]{2,0,1:T(8,128)(2,1)} %param.19) | copy-start | bytes 3145732
  562.2 234.3 %all-gather.18.cloned.1.call-start = ((), (), s32[]{:S(2)}) async-start(), calls=%async_computation.11 | async-start | bytes 5242880 | tf_op jit(solution)/shard_map/all_gather | solution.py:181
  712.4 1.3 copy-start.3
  714.9 242.7 %reduce-scatter.9.cloned.1.call-start = ((), (), s32[]{:S(2)}) async-start(), calls=%async_computation.12 | async-start | bytes 10485760 | tf_op jit(solution)/shard_map/reduce_scatter | solution.py:190
  814.4 232.8 %all-gather.20.cloned.1.call-start = ((), (), s32[]{:S(2)}) async-start(), calls=%async_computation.13 | async-start | bytes 5242880 | tf_op jit(solution)/shard_map/all_gather | solution.py:201
  957.7 3.6 copy-start.2
  957.7 4.1 copy-start.4
  957.7 4.7 copy-start.8
  963.2 1.3 copy-start.6
  963.2 84.0 %copy-start.13 = (bf16[256,1024]{1,0:T(8,128)(2,1)S(1)}, bf16[256,1024]{1,0:T(8,128)(2,1)}, u32[]{:S(2)}) copy-start(bf16[256,1024]{1,0:T(8,128)(2,1)} %all_gather.32) | copy-start | bytes 1572868
  963.3 88.5 %copy-start.14 = (f32[512]{0:T(512)}, f32[512]{0:T(512)S(1)}, u32[]{:S(2)}) copy-start(f32[512]{0:T(512)S(1)} %negate_multiply_fusion.1) | copy-start | bytes 6148
  965.7 399.0 %all-reduce.4.cloned.1.call-start = ((), (), s32[]{:S(2)}) async-start(), calls=%async_computation.15 | async-start | bytes 131072 | tf_op jit(solution)/shard_map/psum | solution.py:287
  1051.8 9.8 copy-start.5
  1100.5 7.6 copy-start
  1159.4 8.2 copy-start
  1219.7 8.2 copy-start
  1279.9 8.2 copy-start
  1303.6 6.3 copy-start.9
  1312.8 130.3 %reduce-scatter.11.cloned.1.call-start = ((), (), s32[]{:S(2)}) async-start(), calls=%async_computation.14 | async-start | bytes 5242880 | tf_op jit(solution)/shard_map/reduce_scatter | solution.py:210
  1320.2 122.8 %copy-start.7 = (f32[512,1,1024]{2,0,1:T(8,128)S(1)}, f32[512,1,1024]{2,0,1:T(8,128)}, u32[]{:S(2)}) copy-start(f32[512,1,1024]{2,0,1:T(8,128)} %copy-done.6) | copy-start | bytes 6291460
  1320.2 122.8 %copy-start.15 = (f32[512]{0:T(512)S(1)}, f32[512]{0:T(512)}, u32[]{:S(2)}) copy-start(f32[512]{0:T(512)} %copy-done.14) | copy-start | bytes 6148
Sparse Core Ops, SparseCore 0:
  10.4 29.8 all-gather.9
  41.8 80.7 all-gather.7
  263.6 143.1 reduce-scatter.4
  408.5 28.3 all-gather.13
  438.9 80.7 all-gather.11
  521.4 26.5 all-gather.15
  562.3 144.6 reduce-scatter.6
  715.1 81.3 all-gather.17
  814.6 143.0 reduce-scatter.8
  965.9 81.3 all-gather.19
  1312.9 51.8 all-reduce.3
  1366.9 76.1 reduce-scatter.10
where the time goes:
time: 1460 us
  waiting for transfers between devices  920 us (63%)
  matrix products  327 us (22%)
  other arithmetic  141 us (10%)
  local copies, waits for them, and re-layouts  36.2 us (2%)
  between operations  14.8 us (1%)
  blocking collectives  14.6 us (1%)
    reduce_scatter x1, waiting for transfers between devices, reduce_down(): lax.psum_scatter(jnp.einsum('nrf,fd->nrd', active, down_full, preferred_e...  144 us
    reduce_scatter x1, waiting for transfers between devices, up_back(): lax.psum_scatter(jnp.einsum('nrf,df->nrd', grad_hidden, up_full, preferre...  143 us
    reduce_scatter x1, waiting for transfers between devices, mix_heads(): lax.psum_scatter(jnp.einsum('nrk,kd->nrd', mixed, out_full, preferred_ele...  143 us
    dot_general x8, matrix products, block_scores(): jnp.einsum('qhd,khd->hqk', query_block, keys_all, preferred_element_type=...  85.1 us
    all_gather x1, waiting for transfers between devices, expand(): lax.all_gather(normed_low, 'tp', axis=0, tiled=True)  82.8 us
    all_gather x1, waiting for transfers between devices, project_inputs(): piece = lax.all_gather(hidden, 'tp', axis=0, tiled=True)  82.3 us
    all_gather x1, waiting for transfers between devices, output_back(): lax.all_gather(grad_low, 'tp', axis=0, tiled=True)  81.4 us
    all_gather x1, waiting for transfers between devices, mixing_back(): lax.all_gather(grad_low, 'tp', axis=0, tiled=True)  81.4 us
  transfers between devices with their start and end apart: 12, of which 12 were waited for; matrix products, arithmetic and copies ran while one was open for 3% of the time, Pallas kernels for 0%

commit v1 on v0

--- a/solution.py
+++ b/solution.py
@@ -1,3 +1,4 @@
+import functools
 from functools import partial
 import jax
 import jax.numpy as jnp
@@ -10,6 +11,13 @@
 QBLOCK = 512
 EPS = 1e-05
 NEG = -1e30
+
+
+def advance_the_patches(vec, ax_name):
+    return jnp.sum(lax.all_gather(vec, ax_name), 0)
+
+
+compute_cubes = functools.partial(advance_the_patches, ax_name="rows")
 
 
 def layer_norm(values, gain, shift):
@@ -284,7 +292,7 @@
     key_local = jnp.sum(key_grads, axis=0).reshape(PREFIX, width)
     value_local = jnp.sum(value_grads, axis=0).reshape(PREFIX, width)
     key_total, value_total = (
-        lax.psum(key_local.astype(jnp.bfloat16), "rows").astype(jnp.float32),
+        compute_cubes(key_local.astype(jnp.bfloat16)).astype(jnp.float32),
         lax.psum(value_local.astype(jnp.bfloat16), "rows").astype(jnp.float32),
     )
     return (result.astype(jnp.bfloat16), grad_input, key_total, value_total)

time: 1460 us -> 1410 us (0.966)
  waiting for transfers between devices: 920 us -> 839 us
  blocking collectives: 14.6 us -> 49.3 us
    psum x1 -> x0, waiting for transfers between devices: 44.5 us -> none  [body(): lax.psum(key_local.astype(jnp.bfloat16), 'rows').astype(jnp.float32)]
    reduce_scatter x1, waiting for transfers between devices: 75.6 us -> 39.1 us  [input_back(): lax.psum_scatter(jnp.einsum('nrje,jde->nrd', piece, qkv_full, preferred_e...]
    psum x0 -> x1, blocking collectives: none -> 25.2 us  [body(): lax.psum(value_local.astype(jnp.bfloat16), 'rows').astype(jnp.float32)]
  transfers between devices with their start and end apart: 12 -> 11, of which waited for: 12 -> 11; matrix products, arithmetic and copies ran while one was open for 3% -> 2% of each run, Pallas kernels for 0% -> 0%
where the time goes in v1:
time: 1410 us
  waiting for transfers between devices  839 us (60%)
  matrix products  327 us (23%)
  other arithmetic  139 us (10%)
  blocking collectives  49.3 us (3%)
  local copies, waits for them, and re-layouts  39 us (3%)
  between operations  14.4 us (1%)
    reduce_scatter x1, waiting for transfers between devices, reduce_down(): lax.psum_scatter(jnp.einsum('nrf,fd->nrd', active, down_full, preferred_e...  144 us
    reduce_scatter x1, waiting for transfers between devices, up_back(): lax.psum_scatter(jnp.einsum('nrf,df->nrd', grad_hidden, up_full, preferre...  143 us
    reduce_scatter x1, waiting for transfers between devices, mix_heads(): lax.psum_scatter(jnp.einsum('nrk,kd->nrd', mixed, out_full, preferred_ele...  143 us
    dot_general x8, matrix products, block_scores(): jnp.einsum('qhd,khd->hqk', query_block, keys_all, preferred_element_type=...  85 us
    all_gather x1, waiting for transfers between devices, expand(): lax.all_gather(normed_low, 'tp', axis=0, tiled=True)  82.8 us
    all_gather x1, waiting for transfers between devices, project_inputs(): piece = lax.all_gather(hidden, 'tp', axis=0, tiled=True)  82.3 us
    all_gather x1, waiting for transfers between devices, mixing_back(): lax.all_gather(grad_low, 'tp', axis=0, tiled=True)  81.4 us
    all_gather x1, waiting for transfers between devices, output_back(): lax.all_gather(grad_low, 'tp', axis=0, tiled=True)  81.4 us
  transfers between devices with their start and end apart: 11, of which 11 were waited for; matrix products, arithmetic and copies ran while one was open for 2% of the time, Pallas kernels for 0%

profile of v1, /device:TPU:0, one launch (start us, length us, event | category | flops | bytes accessed | tf_op | source)
XLA Modules:
  0.0 1409.3 jit_solution(10785871733444868893)
XLA Ops:
  13.4 14.6 %all_gather.36 = bf16[256,1024]{1,0:T(8,128)(2,1)} all-gather(bf16[256,128]{1,0:T(8,128)(2,1)} %param.23), channel_id=1, replica_groups=mesh['rows'=8,'tp'=4] {'rows'}, dimensions={1}, use_global_device_ids=true | all-gather | bytes 589824 | tf_op jit(solution)/shard_map/all_gather | solution.py:142
  28.0 12.3 all-gather.10.cloned.1.call-done
  40.3 82.3 %all-gather.8.cloned.1.call-done = bf16[2048,1,1024]{2,0,1:T(8,128)(2,1)} async-done(((bf16[512,1,1024]{2,0,1:T(8,128)(2,1)}), bf16[2048,1,1024]{2,0,1:T(8,128)(2,1)}) %all-gather.8.cloned.1.call-update) | async-done | bytes 4194320 | tf_op jit(solution)/shard_map/all_gather | solution.py:149
  135.6 120.7 %while.47 = (s32[]{:T(128)}, bf16[4,512,4,64]{1,3,2,0:T(8,128)(2,1)}, f32[4,4,512]{2,1,0:T(4,128)S(1)}, s32[2112]{0:T(1024)S(1)}, s32[4,512]{1,0:T(4,128)S(1)}, ...) while((s32[]{:T(128)}, ...), condition=%wide.region_5.6_spmd, body=%wide.region_2.5_spmd.sunk | while | flops 1162576384 | bytes 59005412 | solution.py:78
  137.2 8.7 fusion.120
  145.9 9.6 fusion.121
  155.5 10.2 fusion.122
  167.3 8.7 fusion.120
  176.1 9.6 fusion.121
  185.6 10.2 fusion.122
  197.4 8.7 fusion.120
  206.2 9.6 fusion.121
  215.8 10.2 fusion.122
  227.5 8.7 fusion.120
  236.3 9.6 fusion.121
  245.9 10.2 fusion.122
  263.9 142.5 %reduce-scatter.5.cloned.1.call-done = f32[512,1,1024]{2,0,1:T(8,128)} async-done(((f32[2048,1,1024]{2,0,1:T(8,128)}), f32[512,1,1024]{2,0,1:T(8,128)}) %reduce-scatter.5.cloned.1.call-update) | async-done | bytes 2097168 | tf_op jit(solution)/shard_map/reduce_scatter | solution.py:169
  411.8 24.9 %all-gather.14.cloned.1.call-done = bf16[1024,1024]{1,0:T(8,128)(2,1)} async-done(((bf16[128,1024]{1,0:T(8,128)(2,1)}), bf16[1024,1024]{1,0:T(8,128)(2,1)}) %all-gather.14.cloned.1.call-update) | async-done | bytes 2097168 | tf_op jit(solution)/shard_map/all_gather | solution.py:143
  436.6 82.8 %all-gather.12.cloned.1.call-done = bf16[2048,1,1024]{2,0,1:T(8,128)(2,1)} async-done(((bf16[512,1,1024]{2,0,1:T(8,128)(2,1)}), bf16[2048,1,1024]{2,0,1:T(8,128)(2,1)}) %all-gather.12.cloned.1.call-update) | async-done | bytes 4194320 | tf_op jit(solution)/shard_map/all_gather | solution.py:160
  519.4 25.3 %fusion.38 = (f32[2048,1024]{1,0:T(8,128)}, f32[2048,1024]{1,0:T(8,128)}) fusion(f32[1024]{0:T(1024)S(1)} %convert_element_type.126, bf16[1024,1024]{1,0:T(8,128)(2,1)} %all-gather.14.cloned.1.call-done, bf16[2048,1,1024]{2,0,1:T(8,128)(2,1)} %all-gather.12.cloned.1.call-done), kind=kOutput, calls=%fused_computation.53 | convolution fusion | flops 4427087872 | bytes 23072768 | tf_op jit(solution)/shard_map/nrd,df->nrf/dot_general | solution.py:158
  547.8 14.1 %convolution_bitcast_fusion.1 = f32[2048,1,1024]{2,0,1:T(8,128)} fusion(bf16[1024,1024]{1,0:T(8,128)(2,1)} %all-gather.16.cloned.1.call-done, f32[2048,1024]{1,0:T(8,128)} %get-tuple-element.346, f32[2048,1024]{1,0:T(8,128)} %get-tuple-element.347, f32[1024]{0:T(1024)S(1)} %convert_element_type.126), kind=kOutput, calls=%fused_computation.72 | convolution fusion | flops 4303355904 | bytes 27267072 | tf_op jit(solution)/shard_map/nrf,fd->nrd/dot_general | solution.py:179
  562.4 144.3 %reduce-scatter.7.cloned.1.call-done = f32[512,1,1024]{2,0,1:T(8,128)} async-done(((f32[2048,1,1024]{2,0,1:T(8,128)}), f32[512,1,1024]{2,0,1:T(8,128)}) %reduce-scatter.7.cloned.1.call-update) | async-done | bytes 2097168 | tf_op jit(solution)/shard_map/reduce_scatter | solution.py:178
  714.7 81.4 %all-gather.18.cloned.1.call-done = bf16[2048,1,1024]{2,0,1:T(8,128)(2,1)} async-done(((bf16[512,1,1024]{2,0,1:T(8,128)(2,1)}), bf16[2048,1,1024]{2,0,1:T(8,128)(2,1)}) %all-gather.18.cloned.1.call-update) | async-done | bytes 4194320 | tf_op jit(solution)/shard_map/all_gather | solution.py:189
  796.2 17.9 %convolution_bitcast_fusion = f32[2048,1,1024]{2,0,1:T(8,128)} fusion(bf16[1024,1024]{1,0:T(8,128)(2,1)} %all-gather.14.cloned.1.call-done, f32[2048,1024]{1,0:T(8,128)} %get-tuple-element.346, f32[2048,1024]{1,0:T(8,128)} %get-tuple-element.347, f32[1024]{0:T(1024)S(1)} %convert_element_type.126, bf16[1024,1024]{1,0:T(8,128)(2,1)} %all-gather.16.cloned.1.call-done, ...), kind=kOutput, calls=%fused_computation.71 | convolution fusion | flops 8621391872 | bytes 33558528 | tf_op jit(solution)/shard_map/nrf,df->nrd/dot_general | solution.py:199
  814.2 143.2 %reduce-scatter.9.cloned.1.call-done = f32[512,1,1024]{2,0,1:T(8,128)} async-done(((f32[2048,1,1024]{2,0,1:T(8,128)}), f32[512,1,1024]{2,0,1:T(8,128)}) %reduce-scatter.9.cloned.1.call-update) | async-done | bytes 2097168 | tf_op jit(solution)/shard_map/reduce_scatter | solution.py:198
  965.5 81.4 %all-gather.20.cloned.1.call-done = bf16[2048,1,1024]{2,0,1:T(8,128)(2,1)} async-done(((bf16[512,1,1024]{2,0,1:T(8,128)(2,1)}), bf16[2048,1,1024]{2,0,1:T(8,128)(2,1)}) %all-gather.20.cloned.1.call-update) | async-done | bytes 4194320 | tf_op jit(solution)/shard_map/all_gather | solution.py:209
  1061.3 240.0 %while.48 = (s32[]{:T(128)}, f32[2112,4,64]{0,2,1:T(8,128)}, f32[2112,4,64]{0,2,1:T(8,128)}, bf16[4,512,4,64]{1,3,2,0:T(8,128)(2,1)}, bf16[4,512,4,64]{1,3,2,0:T...) while((s32[]{:T(128)}, f32[2112,4,64]{0,2,1:T(8,128)}, ...), condition=%wide.region_19.20_spmd.clone, body=%wide.region_17.19_spmd.clone.sunk | while | flops 2813379072 | bytes 179895344 | solution.py:127
  1062.9 9.3 fusion.132
  1072.2 12.5 multiply_reduce_fusion.6
  1084.7 15.5 %multiply_convert_fusion.4 = bf16[4,512,2112]{1,2,0:T(8,128)(2,1)} fusion(f32[4,512,2112]{1,2,0:T(8,128)} %get-tuple-element.472, f32[4,512,2112]{1,2,0:T(8,128)} %fusion.132, f32[4,512]{1,0:T(4,128)S(1)} %get-tuple-element.473), kind=kLoop, calls=%fused_computation.20.clone.1 | loop fusion | flops 12976128 | bytes 43261952 | tf_op jit(solution)/shard_map/while/body/eval_jaxpr/while/body/eval_jaxpr/convert_element_type | solution.py:102
  1110.1 10.2 fusion.134
  1121.9 9.3 fusion.132
  1131.2 12.5 multiply_reduce_fusion.6
  1143.7 15.5 %multiply_convert_fusion.4 = bf16[4,512,2112]{1,2,0:T(8,128)(2,1)} fusion(f32[4,512,2112]{1,2,0:T(8,128)} %get-tuple-element.472, f32[4,512,2112]{1,2,0:T(8,128)} %fusion.132, f32[4,512]{1,0:T(4,128)S(1)} %get-tuple-element.473), kind=kLoop, calls=%fused_computation.20.clone.1 | loop fusion | flops 12976128 | bytes 43261952 | tf_op jit(solution)/shard_map/while/body/eval_jaxpr/while/body/eval_jaxpr/convert_element_type | solution.py:102
  1159.2 8.2 fusion.133
  1169.8 10.8 fusion.134
  1182.2 9.3 fusion.132
  1191.5 12.5 multiply_reduce_fusion.6
  1204.0 15.5 %multiply_convert_fusion.4 = bf16[4,512,2112]{1,2,0:T(8,128)(2,1)} fusion(f32[4,512,2112]{1,2,0:T(8,128)} %get-tuple-element.472, f32[4,512,2112]{1,2,0:T(8,128)} %fusion.132, f32[4,512]{1,0:T(4,128)S(1)} %get-tuple-element.473), kind=kLoop, calls=%fused_computation.20.clone.1 | loop fusion | flops 12976128 | bytes 43261952 | tf_op jit(solution)/shard_map/while/body/eval_jaxpr/while/body/eval_jaxpr/convert_element_type | solution.py:102
  1219.5 8.2 fusion.133
  1230.0 10.8 fusion.134
  1242.4 9.3 fusion.132
  1251.7 12.5 multiply_reduce_fusion.6
  1264.2 15.5 %multiply_convert_fusion.4 = bf16[4,512,2112]{1,2,0:T(8,128)(2,1)} fusion(f32[4,512,2112]{1,2,0:T(8,128)} %get-tuple-element.472, f32[4,512,2112]{1,2,0:T(8,128)} %fusion.132, f32[4,512]{1,0:T(4,128)S(1)} %get-tuple-element.473), kind=kLoop, calls=%fused_computation.20.clone.1 | loop fusion | flops 12976128 | bytes 43261952 | tf_op jit(solution)/shard_map/while/body/eval_jaxpr/while/body/eval_jaxpr/convert_element_type | solution.py:102
  1290.3 10.8 fusion.134
  1322.2 9.4 all_gather.42
  1332.6 25.2 %psum.7 = bf16[64,256]{1,0:T(8,128)(2,1)S(1)} all-reduce(bf16[64,256]{1,0:T(8,128)(2,1)S(1)} %copy.76), channel_id=1, replica_groups=mesh['rows'=8,'tp'=4] {'rows'}, use_global_device_ids=true, to_apply=%region_22.23 | all-reduce | flops 16384 | bytes 65536 | tf_op jit(solution)/shard_map/psum | solution.py:296
  1358.4 39.1 %reduce-scatter.11.cloned.1.call-done = bf16[512,1,1024]{2,0,1:T(8,128)(2,1)} async-done(((bf16[2048,1,1024]{2,0,1:T(8,128)(2,1)}), bf16[512,1,1024]{2,0,1:T(8,128)(2,1)}) %reduce-scatter.11.cloned.1.call-update) | async-done | bytes 1048592 | tf_op jit(solution)/shard_map/reduce_scatter | solution.py:218
  (180 shorter events, 131.1 us)
Async XLA Ops:
  7.2 33.1 %all-gather.10.cloned.1.call-start = ((), (), s32[]{:S(2)}) async-start(), calls=%async_computation.5 | async-start | bytes 1769472 | tf_op jit(solution)/shard_map/all_gather | solution.py:141
  9.0 113.6 %all-gather.8.cloned.1.call-start = ((), (), s32[]{:S(2)}) async-start(), calls=%async_computation.4 | async-start | bytes 5242880 | tf_op jit(solution)/shard_map/all_gather | solution.py:149
  9.7 396.7 %reduce-scatter.5.cloned.1.call-start = ((), (), s32[]{:S(2)}) async-start(), calls=%async_computation.6 | async-start | bytes 10485760 | tf_op jit(solution)/shard_map/reduce_scatter | solution.py:169
  256.3 2.4 copy-start.12
  263.2 0.7 copy-start.16
  263.2 0.7 copy-start.17
  263.2 0.7 copy-start.18
  263.2 143.3 %copy-start.10 = (bf16[512,1,1024]{2,0,1:T(8,128)(2,1)S(1)}, bf16[512,1,1024]{2,0,1:T(8,128)(2,1)}, u32[]{:S(2)}) copy-start(bf16[512,1,1024]{2,0,1:T(8,128)(2,1)} %param.18) | copy-start | bytes 3145732
  263.2 173.4 %all-gather.14.cloned.1.call-start = ((), (), s32[]{:S(2)}) async-start(), calls=%async_computation.8 | async-start | bytes 2359296 | tf_op jit(solution)/shard_map/all_gather | solution.py:143
  263.8 255.6 %all-gather.12.cloned.1.call-start = ((), (), s32[]{:S(2)}) async-start(), calls=%async_computation.7 | async-start | bytes 5242880 | tf_op jit(solution)/shard_map/all_gather | solution.py:160
  408.4 1.3 copy-start.1
  408.4 3.3 copy-start.19
  411.1 136.6 %all-gather.16.cloned.1.call-start = ((), (), s32[]{:S(2)}) async-start(), calls=%async_computation.9 | async-start | bytes 2359296 | tf_op jit(solution)/shard_map/all_gather | solution.py:144
  411.7 295.0 %reduce-scatter.7.cloned.1.call-start = ((), (), s32[]{:S(2)}) async-start(), calls=%async_computation.10 | async-start | bytes 10485760 | tf_op jit(solution)/shard_map/reduce_scatter | solution.py:178
  561.9 147.7 %copy-start.11 = (bf16[512,1,1024]{2,0,1:T(8,128)(2,1)S(1)}, bf16[512,1,1024]{2,0,1:T(8,128)(2,1)}, u32[]{:S(2)}) copy-start(bf16[512,1,1024]{2,0,1:T(8,128)(2,1)} %param.19) | copy-start | bytes 3145732
  561.9 234.3 %all-gather.18.cloned.1.call-start = ((), (), s32[]{:S(2)}) async-start(), calls=%async_computation.11 | async-start | bytes 5242880 | tf_op jit(solution)/shard_map/all_gather | solution.py:189
  712.2 1.3 copy-start.3
  714.7 242.7 %reduce-scatter.9.cloned.1.call-start = ((), (), s32[]{:S(2)}) async-start(), calls=%async_computation.12 | async-start | bytes 10485760 | tf_op jit(solution)/shard_map/reduce_scatter | solution.py:198
  814.2 232.8 %all-gather.20.cloned.1.call-start = ((), (), s32[]{:S(2)}) async-start(), calls=%async_computation.13 | async-start | bytes 5242880 | tf_op jit(solution)/shard_map/all_gather | solution.py:209
  957.4 3.6 copy-start.2
  957.4 4.1 copy-start.4
  957.4 4.7 copy-start.8
  963.0 1.3 copy-start.6
  963.0 84.0 %copy-start.13 = (bf16[256,1024]{1,0:T(8,128)(2,1)S(1)}, bf16[256,1024]{1,0:T(8,128)(2,1)}, u32[]{:S(2)}) copy-start(bf16[256,1024]{1,0:T(8,128)(2,1)} %all_gather.36) | copy-start | bytes 1572868
  963.0 88.5 %copy-start.14 = (f32[512]{0:T(512)}, f32[512]{0:T(512)S(1)}, u32[]{:S(2)}) copy-start(f32[512]{0:T(512)S(1)} %negate_multiply_fusion.1) | copy-start | bytes 6148
  965.5 432.1 %reduce-scatter.11.cloned.1.call-start = ((), (), s32[]{:S(2)}) async-start(), calls=%async_computation.14 | async-start | bytes 5242880 | tf_op jit(solution)/shard_map/reduce_scatter | solution.py:218
  1051.5 9.8 copy-start.5
  1100.2 7.6 copy-start
  1159.2 8.2 copy-start
  1219.5 8.2 copy-start
  1279.7 8.2 copy-start
  1306.5 1.0 copy-start.9
  1322.1 10.4 slice-start
  1322.1 75.5 %copy-start.7 = (f32[512,1,1024]{2,0,1:T(8,128)S(1)}, f32[512,1,1024]{2,0,1:T(8,128)}, u32[]{:S(2)}) copy-start(f32[512,1,1024]{2,0,1:T(8,128)} %copy-done.6) | copy-start | bytes 6291460
  1322.1 75.5 %copy-start.15 = (f32[512]{0:T(512)S(1)}, f32[512]{0:T(512)}, u32[]{:S(2)}) copy-start(f32[512]{0:T(512)} %copy-done.14) | copy-start | bytes 6148
Sparse Core Ops, SparseCore 0:
  10.4 29.8 all-gather.9
  41.8 80.7 all-gather.7
  263.3 143.0 reduce-scatter.4
  408.2 28.3 all-gather.13
  438.6 80.7 all-gather.11
  521.1 26.5 all-gather.15
  562.0 144.6 reduce-scatter.6
  714.8 81.3 all-gather.17
  814.3 143.0 reduce-scatter.8
  965.6 81.3 all-gather.19
  1322.2 75.2 reduce-scatter.10
